TPU v7x, 512 devices: a whole 4x4x16 slice. The times are simulated.
512 devices in a mesh: dp: 32 (over y, x, core), mp: 16 (over z).
Axes of the slice: x: 4, y: 4, z: 16, core: 2. Of those that a mesh axis runs over, the one named last changes fastest.
Arguments:
- tokens: bfloat16 [32768, 8192], P('dp', 'mp'), may hold values from -6 to 6
- value_weight: bfloat16 [8192, 1024], P('mp'), may hold values from -0.0625 to 0.0625
- down_panels: bfloat16 [256, 8192, 64], P('dp', 'mp'), may hold values from -0.0625 to 0.0625
- up_panels: bfloat16 [256, 64, 1024], P('dp'), may hold values from -0.75 to 0.75
- cotangent: bfloat16 [32768, 1024], P(('dp', 'mp')), may hold values from -6 to 6
- block_adapter: int32 [256], replicated, may hold values from 0 to 255, as said below
- adapter_slot: int32 [256], replicated, may hold values from 0 to 255, as said below
Outputs:
- projected: bfloat16 [32768, 1024], P(('dp', 'mp'))
- grad_tokens: bfloat16 [32768, 8192], P('dp', 'mp')
- grad_down: bfloat16 [256, 8192, 64], P('dp', 'mp')
- grad_up: bfloat16 [256, 64, 1024], P('dp')
Inputs may be any that keep to these rules, and one draw needn't show every extreme that they name: `block_adapter`: the 8 blocks of one index of dp name adapters stored on 8 different owners, the owner of slot s being s // 8. `adapter_slot`: A permutation of the adapters.
All inputs are finite; a program needn't handle non-finite values.
Results may differ from a plain program's by a relative error of at most 0.005.
Values may be sent and summed in bfloat16 or wider, within the bound.
A program may use at most 128 MiB of HBM per device.

v0:
```python
import jax
import jax.numpy as jnp
from jax import lax
from jax.sharding import PartitionSpec as P

RANK = 64
BLOCK_ROWS = 128


def per_device(
    tokens, value_weight, down_panels, up_panels, cotangent, block_adapter, adapter_slot
):
    n_owners = lax.axis_size("dp")
    myself = lax.axis_index("dp")
    n_split = lax.axis_size("mp")
    my_part = lax.axis_index("mp")
    rows, width_dev = tokens.shape
    own_rows, kv_full = cotangent.shape
    kv_part = kv_full // n_split
    stored = down_panels.shape[0]
    blocks = rows // BLOCK_ROWS
    hits = block_adapter[:, None] == jnp.arange(adapter_slot.shape[0], dtype=jnp.int32)[None, :]
    slots_all = jnp.sum(jnp.where(hits, adapter_slot[None, :], 0), axis=1)
    owner_all = (slots_all // stored).reshape(n_owners, blocks)
    local_all = (slots_all % stored).reshape(n_owners, blocks)
    mine = owner_all == myself
    wanted = jnp.sum(jnp.where(mine, local_all, 0), axis=1)
    served = jnp.any(mine, axis=1)
    pick_mask = (wanted[:, None] == jnp.arange(stored, dtype=jnp.int32)[None, :]) & served[:, None]
    my_owner = lax.dynamic_index_in_dim(owner_all, myself, 0, keepdims=False)
    select_mask = my_owner[:, None] == jnp.arange(n_owners, dtype=jnp.int32)[None, :]
    up_cols = lax.dynamic_slice_in_dim(up_panels, my_part * kv_part, kv_part, 2)
    both = jnp.concatenate([down_panels, up_cols], axis=1)
    got = lax.all_to_all(
        jnp.take(both, wanted, axis=0), "dp", split_axis=0, concat_axis=0, tiled=True
    )
    mine_got = jnp.take(got, my_owner, axis=0)
    panel_a = mine_got[:, :width_dev]
    panel_b_cols = mine_got[:, width_dev:]
    cot_all = lax.all_gather(cotangent, "mp", axis=0, tiled=True)
    panel_b = lax.all_gather(panel_b_cols, "mp", axis=2, tiled=True)
    token_blocks = tokens.reshape(blocks, BLOCK_ROWS, width_dev)
    partial_value = jnp.dot(tokens, value_weight, preferred_element_type=jnp.float32)
    base = lax.psum_scatter(partial_value, "mp", scatter_dimension=0, tiled=True)
    down_part = jnp.einsum(
        "bnd,bdk->bnk", token_blocks, panel_a, preferred_element_type=jnp.float32
    )
    first_row = my_part * own_rows
    my_down = lax.psum_scatter(
        down_part.reshape(rows, RANK), "mp", scatter_dimension=0, tiled=True
    ).astype(jnp.bfloat16)
    down = lax.all_gather(my_down, "mp", axis=0, tiled=True)
    cot_blocks = cot_all.reshape(blocks, BLOCK_ROWS, kv_full)
    back = jnp.einsum(
        "bnc,bkc->bnk", cot_blocks, panel_b, preferred_element_type=jnp.float32
    ).astype(jnp.bfloat16)
    block_grad_a = jnp.einsum(
        "bnd,bnk->bdk", token_blocks, back, preferred_element_type=jnp.float32
    ).astype(jnp.bfloat16)
    cot_share = lax.dynamic_slice_in_dim(cot_blocks, my_part * kv_part, kv_part, 2)
    block_grad_b = jnp.einsum(
        "bnk,bnc->bkc",
        down.reshape(blocks, BLOCK_ROWS, RANK),
        cot_share,
        preferred_element_type=jnp.float32,
    ).astype(jnp.bfloat16)
    grads = jnp.concatenate([block_grad_a, block_grad_b], axis=1)
    send_g = jnp.einsum(
        "bo,bdk->odk", select_mask.astype(jnp.bfloat16), grads, preferred_element_type=jnp.float32
    ).astype(jnp.bfloat16)
    recv_g = lax.all_to_all(send_g, "dp", split_axis=0, concat_axis=0, tiled=True)
    grad_both = jnp.einsum(
        "ra,rdk->adk", pick_mask.astype(jnp.bfloat16), recv_g, preferred_element_type=jnp.float32
    ).astype(jnp.bfloat16)
    grad_down = grad_both[:, :width_dev]
    grad_up = lax.all_gather(grad_both[:, width_dev:], "mp", axis=2, tiled=True)
    my_up = lax.dynamic_index_in_dim(panel_b, first_row // BLOCK_ROWS, 0, keepdims=False)
    lifted = jnp.dot(my_down, my_up, preferred_element_type=jnp.float32)
    projected = (base + lifted).astype(jnp.bfloat16)
    grad_base = jnp.einsum("nc,dc->nd", cot_all, value_weight, preferred_element_type=jnp.float32)
    through = jnp.einsum("bnk,bdk->bnd", back, panel_a, preferred_element_type=jnp.float32)
    grad_tokens = (grad_base + through.reshape(rows, width_dev)).astype(jnp.bfloat16)
    return (projected, grad_tokens, grad_down, grad_up)


def solution(mesh):
    placed = (
        P("dp", "mp"),
        P("mp", None),
        P("dp", "mp", None),
        P("dp", None, None),
        P(("dp", "mp"), None),
        P(),
        P(),
    )
    return jax.shard_map(
        per_device,
        mesh=mesh,
        in_specs=placed,
        out_specs=(P(("dp", "mp"), None), P("dp", "mp"), P("dp", "mp", None), P("dp", None, None)),
        check_vma=False,
    )
```

profile of v0, /device:TPU:2, one launch (start us, length us, event | category | flops | bytes accessed | tf_op | source)
XLA Modules:
  0.0 442.6 jit_solution(5169202900593899612)
XLA Ops:
  7.2 1.0 select_reduce_fusion
  8.1 0.1 reduce_sum.23
  8.2 0.1 fusion.32
  8.4 0.1 fusion.16
  8.5 1.0 constant_dynamic-slice_fusion
  9.5 0.1 copy.42
  9.7 1.1 pad_maximum_fusion
  10.8 2.4 gather_fusion
  13.2 3.6 broadcast_select_fusion
  16.8 10.3 %all-to-all-start = ((bf16[32,576,64]{1,2,0:T(8,128)(2,1)}), bf16[32,576,64]{1,2,0:T(8,128)(2,1)}, u32[]{:S(2)}, u32[]{:S(2)}) async-start(bf16[32,576,64]{1,2,0:T(8,128)(2,1)} %broadcast_select_fusion), calls=%async_computation.1 | async-start | bytes 5242880 | tf_op jit(solution)/shard_map/all_to_all | solution.py:34
  27.1 0.0 reduce-scatter.7.cloned.1.call-start
  27.2 33.9 %all-to-all-done = bf16[32,576,64]{1,2,0:T(8,128)(2,1)} async-done(((bf16[32,576,64]{1,2,0:T(8,128)(2,1)}), bf16[32,576,64]{1,2,0:T(8,128)(2,1)}, u32[]{:S(2)}, u32[]{:S(2)}) %all-to-all-start) | async-done | bytes 2359328 | tf_op jit(solution)/shard_map/all_to_all | solution.py:34
  61.1 2.4 gather_fusion.1
  63.5 0.1 broadcast_select_fusion.1
  63.6 0.5 convolution_bitcast_fusion
  64.1 1.0 copy.60
  65.1 0.0 reduce-scatter.7.cloned.1.call-update
  65.1 0.0 all-gather.6.cloned.1.call-start
  65.2 0.7 all-gather.6.cloned.1.call-update
  65.9 0.0 all-gather.4.cloned.1.call-start
  65.9 0.7 slice.21
  66.6 0.0 reduce-scatter.5.cloned.1.call-start
  66.7 4.4 fusion.34
  71.1 0.0 all-gather.8.cloned.1.call-start
  71.2 62.2 %reduce-scatter.7.cloned.1.call-done = f32[64,64]{1,0:T(8,128)} async-done(((f32[1024,64]{1,0:T(8,128)}), f32[64,64]{1,0:T(8,128)}) %reduce-scatter.7.cloned.1.call-update) | async-done | bytes 16400
  133.4 0.8 copy.59
  134.2 0.1 copy.45
  134.3 29.0 %all_gather.14 = bf16[1024,64]{1,0:T(8,128)(2,1)S(1)} all-gather(bf16[64,64]{1,0:T(8,128)(2,1)S(1)} %copy.45), channel_id=1, replica_groups=mesh['dp'=32,'mp'=16] {'mp'}, dimensions={0}, use_global_device_ids=true | all-gather | bytes 139264 | tf_op jit(solution)/shard_map/all_gather | solution.py:52
  163.3 43.5 %all-gather.6.cloned.1.call-done = bf16[1024,1024]{1,0:T(8,128)(2,1)} async-done(((bf16[64,1024]{1,0:T(8,128)(2,1)}), bf16[1024,1024]{1,0:T(8,128)(2,1)}) %all-gather.6.cloned.1.call-update) | async-done | bytes 2097168 | tf_op jit(solution)/shard_map/all_gather | solution.py:40
  206.8 1.3 convolution_convert_fusion.2
  208.1 71.3 %all-gather.4.cloned.1.call-done = bf16[8,64,1024]{1,2,0:T(8,128)(2,1)} async-done(((bf16[8,64,64]{1,2,0:T(8,128)(2,1)}), bf16[8,64,1024]{1,2,0:T(8,128)(2,1)}) %all-gather.4.cloned.1.call-update) | async-done | bytes 1048592 | tf_op jit(solution)/shard_map/all_gather | solution.py:41
  279.4 3.1 convolution_convert_fusion.3
  282.5 0.3 fusion.6
  282.8 0.1 pad_maximum_fusion.1
  282.9 1.0 convolution_convert_fusion
  283.9 0.9 copy.50
  284.8 40.2 %all_to_all.10 = bf16[32,576,64]{1,2,0:T(8,128)(2,1)S(1)} all-to-all(bf16[32,576,64]{1,2,0:T(8,128)(2,1)S(1)} %copy.50), channel_id=1, replica_groups=mesh['dp'=32,'mp'=16] {'dp'}, dimensions={0} | all-to-all | bytes 4718592 | tf_op jit(solution)/shard_map/all_to_all | solution.py:71
  325.0 1.8 fusion.3
  326.8 0.7 slice.23
  327.5 0.5 fusion.9
  328.0 0.1 copy-done.2
  328.1 1.1 copy-done.1
  329.2 2.3 fusion.2
  331.5 0.9 copy.52
  332.5 26.8 %reduce-scatter.5.cloned.1.call-done = f32[64,1024]{1,0:T(8,128)} async-done(((f32[1024,1024]{1,0:T(8,128)}), f32[64,1024]{1,0:T(8,128)}) %reduce-scatter.5.cloned.1.call-update) | async-done | bytes 262160 | tf_op jit(solution)/shard_map/reduce_scatter | solution.py:44
  359.2 1.9 fusion.7
  361.2 71.6 %all-gather.8.cloned.1.call-done = bf16[8,64,1024]{1,0,2:T(8,128)(2,1)} async-done(((bf16[8,64,64]{1,0,2:T(8,128)(2,1)}), bf16[8,64,1024]{1,0,2:T(8,128)(2,1)}) %all-gather.8.cloned.1.call-update) | async-done | bytes 1048592 | tf_op jit(solution)/shard_map/all_gather | solution.py:76
  432.8 3.3 copy.53
  (14 shorter events, 0.2 us)
Async XLA Ops:
  7.2 56.5 %copy-start = (bf16[1024,512]{1,0:T(8,128)(2,1)S(1)}, bf16[1024,512]{1,0:T(8,128)(2,1)}, u32[]{:S(2)}) copy-start(bf16[1024,512]{1,0:T(8,128)(2,1)} %param.7) | copy-start | bytes 3145732
  16.8 44.3 %all-to-all-start = ((bf16[32,576,64]{1,2,0:T(8,128)(2,1)}), bf16[32,576,64]{1,2,0:T(8,128)(2,1)}, u32[]{:S(2)}, u32[]{:S(2)}) async-start(bf16[32,576,64]{1,2,0:T(8,128)(2,1)} %broadcast_select_fusion), calls=%async_computation.1 | async-start | bytes 5242880 | tf_op jit(solution)/shard_map/all_to_all | solution.py:34
  27.1 106.3 %reduce-scatter.7.cloned.1.call-start = ((), (), s32[]{:S(2)}) async-start(), calls=%async_computation.8 | async-start | bytes 557056
  65.1 141.6 %all-gather.6.cloned.1.call-start = ((), (), s32[]{:S(2)}) async-start(), calls=%async_computation.6 | async-start | bytes 2228224 | tf_op jit(solution)/shard_map/all_gather | solution.py:40
  65.9 213.5 %all-gather.4.cloned.1.call-start = ((), (), s32[]{:S(2)}) async-start(), calls=%async_computation.5 | async-start | bytes 2228224 | tf_op jit(solution)/shard_map/all_gather | solution.py:41
  66.6 292.6 %reduce-scatter.5.cloned.1.call-start = ((), (), s32[]{:S(2)}) async-start(), calls=%async_computation.4 | async-start | bytes 4456448 | tf_op jit(solution)/shard_map/reduce_scatter | solution.py:44
  71.1 361.6 %all-gather.8.cloned.1.call-start = ((), (), s32[]{:S(2)}) async-start(), calls=%async_computation.7 | async-start | bytes 2228224 | tf_op jit(solution)/shard_map/all_gather | solution.py:76
  326.8 1.3 copy-start.2
  327.5 1.7 copy-start.1
Sparse Core Ops, SparseCore 0:
  65.3 68.0 reduce-scatter.6
  135.7 71.0 all-gather.5
  209.7 69.7 all-gather.3
  282.4 76.8 reduce-scatter.4
  362.0 70.7 all-gather.7
where the time goes:
time: 443 us
  waiting for transfers between devices  310 us (70%)
  blocking collectives  69.2 us (16%)
  matrix products  17 us (4%)
  local copies, waits for them, and re-layouts  15.7 us (4%)
  between operations  14 us (3%)
  starting transfers between devices  10.5 us (2%)
  other arithmetic  6.2 us (1%)
    all_gather x1, waiting for transfers between devices, per_device(): grad_up = lax.all_gather(grad_both[:, width_dev:], 'mp', axis=2, tiled=True)  71.6 us
    all_gather x1, waiting for transfers between devices, per_device(): panel_b = lax.all_gather(panel_b_cols, 'mp', axis=2, tiled=True)  71.3 us
    unnamed x6, waiting for transfers between devices  62.9 us
    all_gather x1, waiting for transfers between devices, per_device(): cot_all = lax.all_gather(cotangent, 'mp', axis=0, tiled=True)  43.5 us
    all_to_all x1, blocking collectives, per_device(): lax.all_to_all(send_g, 'dp', split_axis=0, concat_axis=0, tiled=True)  40.2 us
    all_to_all x1, waiting for transfers between devices, per_device(): lax.all_to_all(jnp.take(both, wanted, axis=0), 'dp', split_axis=0, concat...  33.9 us
    all_gather x1, blocking collectives, per_device(): down = lax.all_gather(my_down, 'mp', axis=0, tiled=True)  29 us
    reduce_scatter x1, waiting for transfers between devices, per_device(): lax.psum_scatter(partial_value, 'mp', scatter_dimension=0, tiled=True)  26.8 us
  transfers between devices with their start and end apart: 6, of which 6 were waited for; matrix products, arithmetic and copies ran while one was open for 5% of the time, Pallas kernels for 0%

commit v1 on v0

--- a/solution.py
+++ b/solution.py
@@ -5,6 +5,17 @@
 
 RANK = 64
 BLOCK_ROWS = 128
+
+
+def gather_by_hops(x, axis, dim):
+    peers = lax.axis_size(axis)
+    right = [(i, (i + 1) % peers) for i in range(peers)]
+    parts = [x]
+    for hop in range(1, peers):
+        parts = [lax.ppermute(parts[0], axis, right), *parts]
+    result = jnp.concatenate(parts, axis=dim)
+    places = (lax.axis_index(axis) + 1) * parts[-1].shape[dim]
+    return jnp.roll(result, places, axis=dim)
 
 
 def per_device(
@@ -37,7 +48,7 @@
     mine_got = jnp.take(got, my_owner, axis=0)
     panel_a = mine_got[:, :width_dev]
     panel_b_cols = mine_got[:, width_dev:]
-    cot_all = lax.all_gather(cotangent, "mp", axis=0, tiled=True)
+    cot_all = gather_by_hops(cotangent, "mp", 0)
     panel_b = lax.all_gather(panel_b_cols, "mp", axis=2, tiled=True)
     token_blocks = tokens.reshape(blocks, BLOCK_ROWS, width_dev)
     partial_value = jnp.dot(tokens, value_weight, preferred_element_type=jnp.float32)

time: 443 us -> 373 us (0.84)
  waiting for transfers between devices: 310 us -> 210 us
  starting transfers between devices: 10.5 us -> 39.1 us
    ppermute x0 -> x15, waiting for transfers between devices: none -> 104 us  [gather_by_hops(): parts = [lax.ppermute(parts[0], axis, right), *parts]]
    all_gather x1, waiting for transfers between devices: 71.3 us -> 0.02 us  [per_device(): panel_b = lax.all_gather(panel_b_cols, 'mp', axis=2, tiled=True)]
    unnamed x6 -> x5, waiting for transfers between devices: 62.9 us -> 0.09 us
    all_gather x1 -> x0, waiting for transfers between devices: 43.5 us -> none  [per_device(): cot_all = lax.all_gather(cotangent, 'mp', axis=0, tiled=True)]
    ppermute x0 -> x15, starting transfers between devices: none -> 28.6 us  [gather_by_hops(): parts = [lax.ppermute(parts[0], axis, right), *parts]]
    reduce_scatter x1, waiting for transfers between devices: 26.8 us -> 0.95 us  [per_device(): lax.psum_scatter(partial_value, 'mp', scatter_dimension=0, tiled=True)]
  transfers between devices with their start and end apart: 6 -> 20, of which waited for: 6 -> 18; matrix products, arithmetic and copies ran while one was open for 5% -> 6% of each run, Pallas kernels for 0% -> 0%
where the time goes in v1:
time: 373 us; the launch traced here: 372 us
  waiting for transfers between devices  210 us (56%)
  blocking collectives  68 us (18%)
  starting transfers between devices  39.1 us (10%)
  matrix products  17.8 us (5%)
  local copies, waits for them, and re-layouts  16 us (4%)
  between operations  14.4 us (4%)
  other arithmetic  6.23 us (2%)
    ppermute x15, waiting for transfers between devices, gather_by_hops(): parts = [lax.ppermute(parts[0], axis, right), *parts]  104 us
    all_gather x1, waiting for transfers between devices, per_device(): grad_up = lax.all_gather(grad_both[:, width_dev:], 'mp', axis=2, tiled=True)  71.5 us
    all_to_all x1, blocking collectives, per_device(): lax.all_to_all(send_g, 'dp', split_axis=0, concat_axis=0, tiled=True)  40.1 us
    all_to_all x1, waiting for transfers between devices, per_device(): lax.all_to_all(jnp.take(both, wanted, axis=0), 'dp', split_axis=0, concat...  33.9 us
    ppermute x15, starting transfers between devices, gather_by_hops(): parts = [lax.ppermute(parts[0], axis, right), *parts]  28.6 us
    all_gather x1, blocking collectives, per_device(): down = lax.all_gather(my_down, 'mp', axis=0, tiled=True)  27.8 us
    all_to_all x1, starting transfers between devices, per_device(): lax.all_to_all(jnp.take(both, wanted, axis=0), 'dp', split_axis=0, concat...  10.3 us
  transfers between devices with their start and end apart: 20, of which 18 were waited for; matrix products, arithmetic and copies ran while one was open for 6% of the time, Pallas kernels for 0%

profile of v1, /device:TPU:2, one launch (start us, length us, event | category | flops | bytes accessed | tf_op | source)
XLA Modules:
  0.0 371.5 jit_solution(7375124786495941900)
XLA Ops:
  8.5 1.0 constant_dynamic-slice_fusion.1
  9.7 1.1 pad_maximum_fusion
  10.8 2.4 gather_fusion
  13.2 3.6 broadcast_select_fusion
  16.8 10.3 %all-to-all-start = ((bf16[32,576,64]{1,2,0:T(8,128)(2,1)}), bf16[32,576,64]{1,2,0:T(8,128)(2,1)}, u32[]{:S(2)}, u32[]{:S(2)}) async-start(bf16[32,576,64]{1,2,0:T(8,128)(2,1)} %broadcast_select_fusion), calls=%async_computation.1 | async-start | bytes 5242880 | tf_op jit(solution)/shard_map/all_to_all | solution.py:45
  27.3 33.9 %all-to-all-done = bf16[32,576,64]{1,2,0:T(8,128)(2,1)} async-done(((bf16[32,576,64]{1,2,0:T(8,128)(2,1)}), bf16[32,576,64]{1,2,0:T(8,128)(2,1)}, u32[]{:S(2)}, u32[]{:S(2)}) %all-to-all-start) | async-done | bytes 2359328 | tf_op jit(solution)/shard_map/all_to_all | solution.py:45
  61.1 2.4 gather_fusion.1
  64.2 1.0 copy.60
  66.0 1.9 collective-permute-start
  67.9 9.7 %collective-permute-done = bf16[64,1024]{1,0:T(8,128)(2,1)S(1)} collective-permute-done((bf16[64,1024]{1,0:T(8,128)(2,1)S(1)}, bf16[64,1024]{1,0:T(8,128)(2,1)S(1)}, u32[]{:S(2)}, u32[]{:S(2)}) %collective-permute-start) | collective-permute-done | bytes 131104 | tf_op jit(solution)/shard_map/ppermute | solution.py:15
  77.6 1.9 collective-permute-start.1
  79.6 6.5 %collective-permute-done.1 = bf16[64,1024]{1,0:T(8,128)(2,1)S(1)} collective-permute-done((bf16[64,1024]{1,0:T(8,128)(2,1)S(1)}, bf16[64,1024]{1,0:T(8,128)(2,1)S(1)}, u32[]{:S(2)}, u32[]{:S(2)}) %collective-permute-start.1) | collective-permute-done | bytes 131104 | tf_op jit(solution)/shard_map/ppermute | solution.py:15
  86.0 1.9 collective-permute-start.2
  88.0 6.3 %collective-permute-done.2 = bf16[64,1024]{1,0:T(8,128)(2,1)S(1)} collective-permute-done((bf16[64,1024]{1,0:T(8,128)(2,1)S(1)}, bf16[64,1024]{1,0:T(8,128)(2,1)S(1)}, u32[]{:S(2)}, u32[]{:S(2)}) %collective-permute-start.2) | collective-permute-done | bytes 131104 | tf_op jit(solution)/shard_map/ppermute | solution.py:15
  94.2 1.9 collective-permute-start.3
  96.2 6.4 %collective-permute-done.3 = bf16[64,1024]{1,0:T(8,128)(2,1)S(1)} collective-permute-done((bf16[64,1024]{1,0:T(8,128)(2,1)S(1)}, bf16[64,1024]{1,0:T(8,128)(2,1)S(1)}, u32[]{:S(2)}, u32[]{:S(2)}) %collective-permute-start.3) | collective-permute-done | bytes 131104 | tf_op jit(solution)/shard_map/ppermute | solution.py:15
  102.6 1.9 collective-permute-start.4
  104.5 7.3 %collective-permute-done.4 = bf16[64,1024]{1,0:T(8,128)(2,1)S(1)} collective-permute-done((bf16[64,1024]{1,0:T(8,128)(2,1)S(1)}, bf16[64,1024]{1,0:T(8,128)(2,1)S(1)}, u32[]{:S(2)}, u32[]{:S(2)}) %collective-permute-start.4) | collective-permute-done | bytes 131104 | tf_op jit(solution)/shard_map/ppermute | solution.py:15
  111.8 1.9 collective-permute-start.5
  113.7 7.6 %collective-permute-done.5 = bf16[64,1024]{1,0:T(8,128)(2,1)S(1)} collective-permute-done((bf16[64,1024]{1,0:T(8,128)(2,1)S(1)}, bf16[64,1024]{1,0:T(8,128)(2,1)S(1)}, u32[]{:S(2)}, u32[]{:S(2)}) %collective-permute-start.5) | collective-permute-done | bytes 131104 | tf_op jit(solution)/shard_map/ppermute | solution.py:15
  121.4 1.9 collective-permute-start.6
  123.3 6.6 %collective-permute-done.6 = bf16[64,1024]{1,0:T(8,128)(2,1)S(1)} collective-permute-done((bf16[64,1024]{1,0:T(8,128)(2,1)S(1)}, bf16[64,1024]{1,0:T(8,128)(2,1)S(1)}, u32[]{:S(2)}, u32[]{:S(2)}) %collective-permute-start.6) | collective-permute-done | bytes 131104 | tf_op jit(solution)/shard_map/ppermute | solution.py:15
  129.9 1.9 collective-permute-start.7
  131.8 6.1 %collective-permute-done.7 = bf16[64,1024]{1,0:T(8,128)(2,1)S(1)} collective-permute-done((bf16[64,1024]{1,0:T(8,128)(2,1)S(1)}, bf16[64,1024]{1,0:T(8,128)(2,1)S(1)}, u32[]{:S(2)}, u32[]{:S(2)}) %collective-permute-start.7) | collective-permute-done | bytes 131104 | tf_op jit(solution)/shard_map/ppermute | solution.py:15
  137.9 1.9 collective-permute-start.8
  139.9 6.1 %collective-permute-done.8 = bf16[64,1024]{1,0:T(8,128)(2,1)S(1)} collective-permute-done((bf16[64,1024]{1,0:T(8,128)(2,1)S(1)}, bf16[64,1024]{1,0:T(8,128)(2,1)S(1)}, u32[]{:S(2)}, u32[]{:S(2)}) %collective-permute-start.8) | collective-permute-done | bytes 131104 | tf_op jit(solution)/shard_map/ppermute | solution.py:15
  146.0 1.9 collective-permute-start.9
  147.9 6.1 %collective-permute-done.9 = bf16[64,1024]{1,0:T(8,128)(2,1)S(1)} collective-permute-done((bf16[64,1024]{1,0:T(8,128)(2,1)S(1)}, bf16[64,1024]{1,0:T(8,128)(2,1)S(1)}, u32[]{:S(2)}, u32[]{:S(2)}) %collective-permute-start.9) | collective-permute-done | bytes 131104 | tf_op jit(solution)/shard_map/ppermute | solution.py:15
  154.1 1.9 collective-permute-start.10
  156.0 4.4 %fusion.34 = f32[1024,1024]{1,0:T(8,128)} fusion(bf16[1024,512]{1,0:T(8,128)(2,1)S(1)} %copy-done, bf16[512,1024]{1,0:T(8,128)(2,1)} %param.8), kind=kOutput, calls=%fused_computation.96 | convolution fusion | flops 1073741824 | bytes 6291456 | tf_op jit(solution)/shard_map/dot_general | solution.py:54
  160.5 2.6 collective-permute-done.10
  163.1 1.9 collective-permute-start.11
  165.0 8.4 %collective-permute-done.11 = bf16[64,1024]{1,0:T(8,128)(2,1)S(1)} collective-permute-done((bf16[64,1024]{1,0:T(8,128)(2,1)S(1)}, bf16[64,1024]{1,0:T(8,128)(2,1)S(1)}, u32[]{:S(2)}, u32[]{:S(2)}) %collective-permute-start.11) | collective-permute-done | bytes 131104 | tf_op jit(solution)/shard_map/ppermute | solution.py:15
  173.4 1.9 collective-permute-start.12
  175.3 9.2 %collective-permute-done.12 = bf16[64,1024]{1,0:T(8,128)(2,1)S(1)} collective-permute-done((bf16[64,1024]{1,0:T(8,128)(2,1)S(1)}, bf16[64,1024]{1,0:T(8,128)(2,1)S(1)}, u32[]{:S(2)}, u32[]{:S(2)}) %collective-permute-start.12) | collective-permute-done | bytes 131104 | tf_op jit(solution)/shard_map/ppermute | solution.py:15
  184.5 1.9 collective-permute-start.13
  186.4 7.8 %collective-permute-done.13 = bf16[64,1024]{1,0:T(8,128)(2,1)S(1)} collective-permute-done((bf16[64,1024]{1,0:T(8,128)(2,1)S(1)}, bf16[64,1024]{1,0:T(8,128)(2,1)S(1)}, u32[]{:S(2)}, u32[]{:S(2)}) %collective-permute-start.13) | collective-permute-done | bytes 131104 | tf_op jit(solution)/shard_map/ppermute | solution.py:15
  194.2 1.9 collective-permute-start.14
  196.2 6.8 %collective-permute-done.14 = bf16[64,1024]{1,0:T(8,128)(2,1)S(1)} collective-permute-done((bf16[64,1024]{1,0:T(8,128)(2,1)S(1)}, bf16[64,1024]{1,0:T(8,128)(2,1)S(1)}, u32[]{:S(2)}, u32[]{:S(2)}) %collective-permute-start.14) | collective-permute-done | bytes 131104 | tf_op jit(solution)/shard_map/ppermute | solution.py:15
  204.8 27.8 %all_gather.10 = bf16[1024,64]{1,0:T(8,128)(2,1)S(1)} all-gather(bf16[64,64]{1,0:T(8,128)(2,1)S(1)} %copy.45), channel_id=1, replica_groups=mesh['dp'=32,'mp'=16] {'mp'}, dimensions={0}, use_global_device_ids=true | all-gather | bytes 139264 | tf_op jit(solution)/shard_map/all_gather | solution.py:63
  233.0 2.5 convolution_convert_fusion.3
  237.7 40.1 %all_to_all.10 = bf16[32,576,64]{1,2,0:T(8,128)(2,1)S(1)} all-to-all(bf16[32,576,64]{1,2,0:T(8,128)(2,1)S(1)} %copy.50), channel_id=1, replica_groups=mesh['dp'=32,'mp'=16] {'dp'}, dimensions={0} | all-to-all | bytes 4718592 | tf_op jit(solution)/shard_map/all_to_all | solution.py:82
  277.9 1.8 fusion.3
  281.3 1.5 fusion.9
  282.8 3.5 fusion.2
  288.3 1.9 fusion.7
  290.2 71.5 %all-gather.5.cloned.1.call-done = bf16[8,64,1024]{1,0,2:T(8,128)(2,1)} async-done(((bf16[8,64,64]{1,0,2:T(8,128)(2,1)}), bf16[8,64,1024]{1,0,2:T(8,128)(2,1)}) %all-gather.5.cloned.1.call-update) | async-done | bytes 1048592 | tf_op jit(solution)/shard_map/all_gather | solution.py:87
  361.7 3.3 copy.53
  (77 shorter events, 10.6 us)
Async XLA Ops:
  7.2 56.5 %copy-start = (bf16[1024,512]{1,0:T(8,128)(2,1)S(1)}, bf16[1024,512]{1,0:T(8,128)(2,1)}, u32[]{:S(2)}) copy-start(bf16[1024,512]{1,0:T(8,128)(2,1)} %param.7) | copy-start | bytes 3145732
  16.8 44.3 %all-to-all-start = ((bf16[32,576,64]{1,2,0:T(8,128)(2,1)}), bf16[32,576,64]{1,2,0:T(8,128)(2,1)}, u32[]{:S(2)}, u32[]{:S(2)}) async-start(bf16[32,576,64]{1,2,0:T(8,128)(2,1)} %broadcast_select_fusion), calls=%async_computation.1 | async-start | bytes 5242880 | tf_op jit(solution)/shard_map/all_to_all | solution.py:45
  27.1 38.9 %copy-start.3 = (bf16[64,1024]{1,0:T(8,128)(2,1)S(1)}, bf16[64,1024]{1,0:T(8,128)(2,1)}, u32[]{:S(2)}) copy-start(bf16[64,1024]{1,0:T(8,128)(2,1)} %param.11) | copy-start | bytes 393220
  27.2 176.6 %reduce-scatter.7.cloned.1.call-start = ((), (), s32[]{:S(2)}) async-start(), calls=%async_computation.7 | async-start | bytes 557056
  63.7 96.7 %copy-start.1 = (bf16[8,576,64]{1,2,0:T(8,128)(2,1)}, bf16[8,576,64]{1,2,0:T(8,128)(2,1)S(1)}, u32[]{:S(2)}) copy-start(bf16[8,576,64]{1,2,0:T(8,128)(2,1)S(1)} %broadcast_select_fusion.1) | copy-start | bytes 1769476
  65.2 167.8 %all-gather.3.cloned.1.call-start = ((), (), s32[]{:S(2)}) async-start(), calls=%async_computation.5 | async-start | bytes 2228224 | tf_op jit(solution)/shard_map/all_gather | solution.py:52
  66.0 222.3 %reduce-scatter.5.cloned.1.call-start = ((), (), s32[]{:S(2)}) async-start(), calls=%async_computation.4 | async-start | bytes 4456448 | tf_op jit(solution)/shard_map/reduce_scatter | solution.py:55
  66.0 11.6 %collective-permute-start = (bf16[64,1024]{1,0:T(8,128)(2,1)S(1)}, bf16[64,1024]{1,0:T(8,128)(2,1)S(1)}, u32[]{:S(2)}, u32[]{:S(2)}) collective-permute-start(bf16[64,1024]{1,0:T(8,128)(2,1)S(1)} %copy-done.3), channel_id=1, source_target_pairs={{0,1},{1,2},{2,3},{3,4},{4,5},{5,6},{6,7},{7,8},{8,9},{9,10},{10,1... | collective-permute-start | bytes 393224 | tf_op jit(solution)/shard_map/ppermute | solution.py:15
  77.6 8.4 %collective-permute-start.1 = (bf16[64,1024]{1,0:T(8,128)(2,1)S(1)}, bf16[64,1024]{1,0:T(8,128)(2,1)S(1)}, u32[]{:S(2)}, u32[]{:S(2)}) collective-permute-start(bf16[64,1024]{1,0:T(8,128)(2,1)S(1)} %collective-permute-done), channel_id=1, source_target_pairs={{0,1},{1,2},{2,3},{3,4},{4,5},{5,6},{6,7},{7,8},{8,9},{9,10},{10,1... | collective-permute-start | bytes 393224 | tf_op jit(solution)/shard_map/ppermute | solution.py:15
  86.0 8.2 %collective-permute-start.2 = (bf16[64,1024]{1,0:T(8,128)(2,1)S(1)}, bf16[64,1024]{1,0:T(8,128)(2,1)S(1)}, u32[]{:S(2)}, u32[]{:S(2)}) collective-permute-start(bf16[64,1024]{1,0:T(8,128)(2,1)S(1)} %collective-permute-done.1), channel_id=1, source_target_pairs={{0,1},{1,2},{2,3},{3,4},{4,5},{5,6},{6,7},{7,8},{8,9},{9,10},{10,1... | collective-permute-start | bytes 393224 | tf_op jit(solution)/shard_map/ppermute | solution.py:15
  94.2 8.3 %collective-permute-start.3 = (bf16[64,1024]{1,0:T(8,128)(2,1)S(1)}, bf16[64,1024]{1,0:T(8,128)(2,1)S(1)}, u32[]{:S(2)}, u32[]{:S(2)}) collective-permute-start(bf16[64,1024]{1,0:T(8,128)(2,1)S(1)} %collective-permute-done.2), channel_id=1, source_target_pairs={{0,1},{1,2},{2,3},{3,4},{4,5},{5,6},{6,7},{7,8},{8,9},{9,10},{10,1... | collective-permute-start | bytes 393224 | tf_op jit(solution)/shard_map/ppermute | solution.py:15
  102.6 9.3 %collective-permute-start.4 = (bf16[64,1024]{1,0:T(8,128)(2,1)S(1)}, bf16[64,1024]{1,0:T(8,128)(2,1)S(1)}, u32[]{:S(2)}, u32[]{:S(2)}) collective-permute-start(bf16[64,1024]{1,0:T(8,128)(2,1)S(1)} %collective-permute-done.3), channel_id=1, source_target_pairs={{0,1},{1,2},{2,3},{3,4},{4,5},{5,6},{6,7},{7,8},{8,9},{9,10},{10,1... | collective-permute-start | bytes 393224 | tf_op jit(solution)/shard_map/ppermute | solution.py:15
  111.8 9.5 %collective-permute-start.5 = (bf16[64,1024]{1,0:T(8,128)(2,1)S(1)}, bf16[64,1024]{1,0:T(8,128)(2,1)S(1)}, u32[]{:S(2)}, u32[]{:S(2)}) collective-permute-start(bf16[64,1024]{1,0:T(8,128)(2,1)S(1)} %collective-permute-done.4), channel_id=1, source_target_pairs={{0,1},{1,2},{2,3},{3,4},{4,5},{5,6},{6,7},{7,8},{8,9},{9,10},{10,1... | collective-permute-start | bytes 393224 | tf_op jit(solution)/shard_map/ppermute | solution.py:15
  121.4 8.5 %collective-permute-start.6 = (bf16[64,1024]{1,0:T(8,128)(2,1)S(1)}, bf16[64,1024]{1,0:T(8,128)(2,1)S(1)}, u32[]{:S(2)}, u32[]{:S(2)}) collective-permute-start(bf16[64,1024]{1,0:T(8,128)(2,1)S(1)} %collective-permute-done.5), channel_id=1, source_target_pairs={{0,1},{1,2},{2,3},{3,4},{4,5},{5,6},{6,7},{7,8},{8,9},{9,10},{10,1... | collective-permute-start | bytes 393224 | tf_op jit(solution)/shard_map/ppermute | solution.py:15
  129.9 8.1 %collective-permute-start.7 = (bf16[64,1024]{1,0:T(8,128)(2,1)S(1)}, bf16[64,1024]{1,0:T(8,128)(2,1)S(1)}, u32[]{:S(2)}, u32[]{:S(2)}) collective-permute-start(bf16[64,1024]{1,0:T(8,128)(2,1)S(1)} %collective-permute-done.6), channel_id=1, source_target_pairs={{0,1},{1,2},{2,3},{3,4},{4,5},{5,6},{6,7},{7,8},{8,9},{9,10},{10,1... | collective-permute-start | bytes 393224 | tf_op jit(solution)/shard_map/ppermute | solution.py:15
  137.9 8.1 %collective-permute-start.8 = (bf16[64,1024]{1,0:T(8,128)(2,1)S(1)}, bf16[64,1024]{1,0:T(8,128)(2,1)S(1)}, u32[]{:S(2)}, u32[]{:S(2)}) collective-permute-start(bf16[64,1024]{1,0:T(8,128)(2,1)S(1)} %collective-permute-done.7), channel_id=1, source_target_pairs={{0,1},{1,2},{2,3},{3,4},{4,5},{5,6},{6,7},{7,8},{8,9},{9,10},{10,1... | collective-permute-start | bytes 393224 | tf_op jit(solution)/shard_map/ppermute | solution.py:15
  146.0 8.1 %collective-permute-start.9 = (bf16[64,1024]{1,0:T(8,128)(2,1)S(1)}, bf16[64,1024]{1,0:T(8,128)(2,1)S(1)}, u32[]{:S(2)}, u32[]{:S(2)}) collective-permute-start(bf16[64,1024]{1,0:T(8,128)(2,1)S(1)} %collective-permute-done.8), channel_id=1, source_target_pairs={{0,1},{1,2},{2,3},{3,4},{4,5},{5,6},{6,7},{7,8},{8,9},{9,10},{10,1... | collective-permute-start | bytes 393224 | tf_op jit(solution)/shard_map/ppermute | solution.py:15
  154.1 9.0 %collective-permute-start.10 = (bf16[64,1024]{1,0:T(8,128)(2,1)S(1)}, bf16[64,1024]{1,0:T(8,128)(2,1)S(1)}, u32[]{:S(2)}, u32[]{:S(2)}) collective-permute-start(bf16[64,1024]{1,0:T(8,128)(2,1)S(1)} %collective-permute-done.9), channel_id=1, source_target_pairs={{0,1},{1,2},{2,3},{3,4},{4,5},{5,6},{6,7},{7,8},{8,9},{9,10},{10,1... | collective-permute-start | bytes 393224 | tf_op jit(solution)/shard_map/ppermute | solution.py:15
  160.4 201.3 %all-gather.5.cloned.1.call-start = ((), (), s32[]{:S(2)}) async-start(), calls=%async_computation.6 | async-start | bytes 2228224 | tf_op jit(solution)/shard_map/all_gather | solution.py:87
  163.1 10.3 %collective-permute-start.11 = (bf16[64,1024]{1,0:T(8,128)(2,1)S(1)}, bf16[64,1024]{1,0:T(8,128)(2,1)S(1)}, u32[]{:S(2)}, u32[]{:S(2)}) collective-permute-start(bf16[64,1024]{1,0:T(8,128)(2,1)S(1)} %collective-permute-done.10), channel_id=1, source_target_pairs={{0,1},{1,2},{2,3},{3,4},{4,5},{5,6},{6,7},{7,8},{8,9},{9,10},{10,1... | collective-permute-start | bytes 393224 | tf_op jit(solution)/shard_map/ppermute | solution.py:15
  173.4 11.1 %collective-permute-start.12 = (bf16[64,1024]{1,0:T(8,128)(2,1)S(1)}, bf16[64,1024]{1,0:T(8,128)(2,1)S(1)}, u32[]{:S(2)}, u32[]{:S(2)}) collective-permute-start(bf16[64,1024]{1,0:T(8,128)(2,1)S(1)} %collective-permute-done.11), channel_id=1, source_target_pairs={{0,1},{1,2},{2,3},{3,4},{4,5},{5,6},{6,7},{7,8},{8,9},{9,10},{10,1... | collective-permute-start | bytes 393224 | tf_op jit(solution)/shard_map/ppermute | solution.py:15
  184.5 9.7 %collective-permute-start.13 = (bf16[64,1024]{1,0:T(8,128)(2,1)S(1)}, bf16[64,1024]{1,0:T(8,128)(2,1)S(1)}, u32[]{:S(2)}, u32[]{:S(2)}) collective-permute-start(bf16[64,1024]{1,0:T(8,128)(2,1)S(1)} %collective-permute-done.12), channel_id=1, source_target_pairs={{0,1},{1,2},{2,3},{3,4},{4,5},{5,6},{6,7},{7,8},{8,9},{9,10},{10,1... | collective-permute-start | bytes 393224 | tf_op jit(solution)/shard_map/ppermute | solution.py:15
  194.2 8.8 %collective-permute-start.14 = (bf16[64,1024]{1,0:T(8,128)(2,1)S(1)}, bf16[64,1024]{1,0:T(8,128)(2,1)S(1)}, u32[]{:S(2)}, u32[]{:S(2)}) collective-permute-start(bf16[64,1024]{1,0:T(8,128)(2,1)S(1)} %collective-permute-done.13), channel_id=1, source_target_pairs={{0,1},{1,2},{2,3},{3,4},{4,5},{5,6},{6,7},{7,8},{8,9},{9,10},{10,1... | collective-permute-start | bytes 393224 | tf_op jit(solution)/shard_map/ppermute | solution.py:15
  279.7 0.9 copy-start.2
  282.8 3.6 slice-start
Sparse Core Ops, SparseCore 0:
  65.3 68.5 reduce-scatter.6
  136.8 71.8 all-gather.2
  211.8 76.4 reduce-scatter.4
  290.4 71.2 all-gather.4
